TPU v7x, 256 devices: a whole 4x4x8 slice. The times are simulated.
256 devices in a mesh: mem: 64 (over z, x_lo, y), band: 4 (over x_hi, core).
Axes of the slice: x: 4 (x_hi: 2, x_lo: 2; x = x_hi * 2 + x_lo), y: 4, z: 8, core: 2. Of those that a mesh axis runs over, the one named last changes fastest.
Arguments:
- alpha: bfloat16 [128, 4, 320, 720], P('mem', None, 'band'), may hold values from -6 to 6
- static_ctl: bfloat16 [4, 320, 720], P(None, 'band'), may hold values from -6 to 6
- perturbations: bfloat16 [128, 4, 320, 720], P('mem', None, None, 'band'), may hold values from -16 to 16
- static_std: float32 [4, 320, 720], P(None, None, 'band'), may hold values from 0.5 to 2
- lon_root: bfloat16 [720, 720], replicated, may hold values from -0.11 to 1.11
- lat_root: bfloat16 [320, 320], replicated, may hold values from -0.11 to 1.11
- jacobian: bfloat16 [32, 4, 320, 720], P(None, None, 'mem', 'band'), may hold values from -3 to 3
- obs_count: int32 [320, 720], P('mem', 'band'), may hold values from 1 to 6
- channel_mask: int32 [32, 320, 720], P(None, 'mem', 'band'), may hold values 0 or 1
- channel_error: float32 [32], replicated, may hold values from 1 to 2
- member_weight: int32 [128], replicated, may hold values from 1 to 4
Outputs:
- grad_alpha: float32 [128, 4, 320, 720], P('mem', None, 'band')
- grad_static: float32 [4, 320, 720], P(None, 'band')
All inputs are finite; a program needn't handle non-finite values. No bound on the sum of `channel_mask` on one device may be relied on, other than what follows from the above.
Results may differ from a plain program's by a relative error of at most 0.0055.
Values may be sent and summed in bfloat16 or wider, within the bound.
A program may use at most 64 MiB of HBM per device.

v0:
```python
import jax
import jax.numpy as jnp
from jax import lax
from jax.sharding import PartitionSpec as P


def in_blocks(x, dim, devices):
    lengths = x.shape
    pieces = x.reshape(*lengths[:dim], devices, lengths[dim] // devices, *lengths[dim + 1 :])
    return jnp.moveaxis(pieces, dim, 0)


def sum_at_owner(x, axis, dim):
    pieces = in_blocks(x, dim, lax.axis_size(axis))
    arrived = lax.all_to_all(pieces, axis, split_axis=0, concat_axis=0, tiled=True)
    return arrived.sum(axis=0)


def laid_out(pieces, dim):
    lengths = list(pieces.shape[1:])
    lengths[dim] *= pieces.shape[0]
    return jnp.moveaxis(pieces, 0, dim).reshape(lengths)


def from_everyone(x, axis):
    devices = lax.axis_size(axis)
    return lax.all_to_all(jnp.broadcast_to(x[None], (devices, *x.shape)), axis, 0, 0, tiled=True)


def collect(x, axis, dim):
    return laid_out(from_everyone(x, axis), dim)


def shards(
    alpha,
    static_ctl,
    perturbations,
    static_std,
    lon_root,
    lat_root,
    jacobian,
    obs_count,
    channel_mask,
    channel_error,
    member_weight,
):
    members = alpha.shape[0]
    rows = jacobian.shape[2]
    rank = lax.axis_index("mem")
    weights = member_weight.astype(jnp.float32)
    coef = weights / jnp.sqrt(jnp.sum(weights * weights))
    own_coef = lax.dynamic_slice_in_dim(coef, rank * members, members, 0)
    fields = jnp.concatenate([alpha, static_ctl[None]], axis=0)
    along_lon = jnp.dot(fields, lon_root, preferred_element_type=jnp.float32).astype(jnp.bfloat16)
    regrouped = lax.all_to_all(along_lon, "band", split_axis=3, concat_axis=2, tiled=True)
    along_lat = jnp.einsum("ij,msjk->msik", lat_root, regrouped, preferred_element_type=jnp.float32)
    member_lat = along_lat[:members]
    own_static = lax.dynamic_slice_in_dim(along_lat[members], rank * rows, rows, 1)
    scaled = 0.8 * own_coef
    ensemble_term = jnp.sum(
        scaled[:, None, None, None] * perturbations.astype(jnp.float32) * member_lat, axis=0
    )
    own_sum = sum_at_owner(ensemble_term, "mem", 1)
    own_std = lax.dynamic_slice_in_dim(static_std, rank * rows, rows, 1)
    increment = own_sum + 0.6 * own_std * own_static
    obs_weight = (
        channel_mask.astype(jnp.float32)
        * obs_count.astype(jnp.float32)[None]
        / (channel_error * channel_error)[:, None, None]
    )
    jac_full = jacobian.astype(jnp.float32)
    radiance = jnp.sum(jac_full * increment[None], axis=1)
    obs_gradient = jnp.sum(jac_full * (obs_weight * radiance)[:, None], axis=0).astype(jnp.bfloat16)
    band_gradient = collect(obs_gradient, "mem", 1).astype(jnp.float32)
    member_adjoint = (
        scaled[:, None, None, None] * perturbations.astype(jnp.float32) * band_gradient[None]
    ).astype(jnp.bfloat16)
    static_adjoint = (0.6 * static_std * band_gradient).astype(jnp.bfloat16)
    adjoints = jnp.concatenate([member_adjoint, static_adjoint[None]], axis=0)
    back_lat = jnp.einsum(
        "ji,msjk->msik", lat_root, adjoints, preferred_element_type=jnp.float32
    ).astype(jnp.bfloat16)
    returned = lax.all_to_all(back_lat, "band", split_axis=2, concat_axis=3, tiled=True)
    back_lon = jnp.einsum("msil,jl->msij", returned, lon_root, preferred_element_type=jnp.float32)
    grad_alpha = alpha.astype(jnp.float32) + back_lon[:members]
    grad_static = static_ctl.astype(jnp.float32) + back_lon[members]
    return (grad_alpha, grad_static)


def solution(mesh):
    in_specs = (
        P("mem", None, "band", None),
        P(None, "band", None),
        P("mem", None, None, "band"),
        P(None, None, "band"),
        P(),
        P(),
        P(None, None, "mem", "band"),
        P("mem", "band"),
        P(None, "mem", "band"),
        P(),
        P(),
    )
    out_specs = (P("mem", None, "band", None), P(None, "band", None))
    return jax.shard_map(shards, mesh=mesh, in_specs=in_specs, out_specs=out_specs, check_vma=False)
```

profile of v0, /device:TPU:1, one launch (start us, length us, event | category | flops | bytes accessed | tf_op | source)
XLA Modules:
  0.0 176.1 jit_solution(13423768554717504345)
XLA Ops:
  0.6 1.2 copy-done
  1.9 2.7 %convolution_convert_fusion.1 = bf16[3,4,80,720]{3,2,1,0:T(8,128)(2,1)S(1)} fusion(bf16[1,4,80,720]{3,2,1,0:T(8,128)(2,1)} %bitcast.49, bf16[2,4,80,720]{3,2,1,0:T(8,128)(2,1)} %param.11, bf16[720,720]{1,0:T(8,128)(2,1)S(1)} %copy-done), kind=kOutput, calls=%fused_computation.10 | convolution fusion | flops 996710400 | bytes 3801600 | tf_op jit(solution)/shard_map/dot_general | solution.py:54
  4.6 3.2 %copy.32 = bf16[3,4,80,720]{2,1,0,3:T(4,128)(2,1)} copy(bf16[3,4,80,720]{3,2,1,0:T(8,128)(2,1)S(1)} %convolution_convert_fusion.1) | data formatting | bytes 2764800 | tf_op jit(solution)/shard_map/convert_element_type | solution.py:54
  7.8 7.0 %all-to-all-start = ((bf16[3,4,80,720]{2,1,0,3:T(4,128)(2,1)}), bf16[3,4,80,720]{2,1,0,3:T(4,128)(2,1)S(1)}, u32[]{:S(2)}, u32[]{:S(2)}) async-start(bf16[3,4,80,720]{2,1,0,3:T(4,128)(2,1)} %copy.32), calls=%async_computation | async-start | bytes 4423680 | tf_op jit(solution)/shard_map/all_to_all | solution.py:55
  16.2 26.2 %all-to-all-done = bf16[3,4,80,720]{2,1,0,3:T(4,128)(2,1)S(1)} async-done(((bf16[3,4,80,720]{2,1,0,3:T(4,128)(2,1)}), bf16[3,4,80,720]{2,1,0,3:T(4,128)(2,1)S(1)}, u32[]{:S(2)}, u32[]{:S(2)}) %all-to-all-start) | async-done | bytes 1382432 | tf_op jit(solution)/shard_map/all_to_all | solution.py:55
  42.3 3.8 %copy.33 = bf16[3,4,80,4,180]{4,2,3,1,0:T(8,128)(2,1)} copy(bf16[3,4,80,4,180]{2,1,0,4,3:T(4,128)(2,1)S(1)} %bitcast.44) | data formatting | bytes 2764800 | tf_op jit(solution)/shard_map/all_to_all | solution.py:55
  46.1 3.3 %convolution_bitcast_fusion = f32[3,4,320,180]{2,3,1,0:T(8,128)S(1)} fusion(bf16[3,4,320,180]{3,2,1,0:T(8,128)(2,1)} %bitcast.46, bf16[320,320]{1,0:T(8,128)(2,1)} %param.16), kind=kOutput, calls=%fused_computation.5 | convolution fusion | flops 442368000 | bytes 4352000 | tf_op jit(solution)/shard_map/ij,msjk->msik/dot_general | solution.py:56
  49.4 1.7 copy-done.1
  51.5 1.5 copy.35
  53.0 11.1 %all-to-all-start.1 = ((f32[64,4,5,180]{3,1,2,0:T(4,128)}), f32[64,4,5,180]{3,1,2,0:T(4,128)S(1)}, u32[]{:S(2)}, u32[]{:S(2)}) async-start(f32[64,4,5,180]{3,1,2,0:T(4,128)} %bitcast.47), calls=%async_computation.1 | async-start | bytes 2621440 | tf_op jit(solution)/shard_map/all_to_all | solution.py:15
  64.7 2.1 %constant_dynamic-slice_fusion.1 = f32[4,5,180]{1,0,2:T(4,128)} fusion(f32[4,320,180]{1,0,2:T(4,128)} %param.14, s32[]{:T(128)S(6)} %select_n.8), kind=kLoop, calls=%fused_computation.38 | loop fusion | bytes 28804 | tf_op jit(solution)/shard_map/dynamic_slice | solution.py:64
  66.8 1.9 %copy.47 = f32[4,5,180]{2,0,1:T(4,128)} copy(f32[4,5,180]{1,0,2:T(4,128)} %constant_dynamic-slice_fusion.1) | data formatting | bytes 28800
  69.6 1.2 copy.37
  70.8 24.6 %all-to-all-done.1 = f32[64,4,5,180]{3,1,2,0:T(4,128)S(1)} async-done(((f32[64,4,5,180]{3,1,2,0:T(4,128)}), f32[64,4,5,180]{3,1,2,0:T(4,128)S(1)}, u32[]{:S(2)}, u32[]{:S(2)}) %all-to-all-start.1) | async-done | bytes 921632 | tf_op jit(solution)/shard_map/all_to_all | solution.py:15
  96.7 24.1 %all_to_all.46 = bf16[64,4,5,180]{3,1,2,0:T(4,128)(2,1)S(1)} all-to-all(bf16[64,4,5,180]{3,1,2,0:T(4,128)(2,1)S(1)} %broadcast_in_dim.7), channel_id=1, replica_groups=mesh['mem'=64,'band'=4] {'mem'}, dimensions={0} | all-to-all | bytes 921600 | tf_op jit(solution)/shard_map/all_to_all | solution.py:27
  121.9 1.5 fusion.18
  124.4 2.5 %fusion.4 = bf16[3,4,320,180]{2,3,1,0:T(8,128)(2,1)} fusion(bf16[1,4,320,180]{2,3,1,0:T(8,128)(2,1)S(1)} %fusion.18, bf16[2,4,320,180]{2,3,1,0:T(8,128)(2,1)S(1)} %multiply_convert_fusion, bf16[320,320]{1,0:T(8,128)(2,1)S(1)} %copy-done.7), kind=kOutput, calls=%fused_computation.11 | convolution fusion | flops 443750400 | bytes 2969600 | tf_op jit(solution)/shard_map/ji,msjk->msik/dot_general | solution.py:80
  127.0 6.7 %copy.41 = bf16[3,4,320,180]{3,1,0,2:T(4,128)(2,1)S(1)} copy(bf16[3,4,320,180]{2,3,1,0:T(8,128)(2,1)} %fusion.4) | data formatting | bytes 2764800 | tf_op jit(solution)/shard_map/convert_element_type | solution.py:82
  133.7 32.7 %all_to_all.47 = bf16[3,4,320,180]{3,1,0,2:T(4,128)(2,1)S(1)} all-to-all(bf16[3,4,320,180]{3,1,0,2:T(4,128)(2,1)S(1)} %copy.41), channel_id=1, replica_groups=mesh['mem'=64,'band'=4] {'band'}, dimensions={2} | all-to-all | bytes 2764800 | tf_op jit(solution)/shard_map/all_to_all | solution.py:83
  166.7 1.0 copy.43
  167.7 2.5 %all_to_all.41 = bf16[3,4,80,720]{3,2,1,0:T(8,128)(2,1)} reshape(bf16[3,4,80,4,180]{4,3,2,1,0:T(4,128)(2,1)S(1)} %copy.43) | data formatting | bytes 2764800 | tf_op jit(solution)/shard_map/all_to_all | solution.py:83
  170.2 2.8 %fusion.12 = f32[3,4,80,720]{3,2,1,0:T(8,128)S(1)} fusion(bf16[3,4,80,720]{3,2,1,0:T(8,128)(2,1)} %all_to_all.41, bf16[720,720]{1,0:T(8,128)(2,1)S(1)} %copy-done), kind=kOutput, calls=%fused_computation.18 | convolution fusion | flops 995328000 | bytes 5184000 | tf_op jit(solution)/shard_map/msil,jl->msij/dot_general | solution.py:84
  173.0 1.0 fusion.15
  174.6 1.5 slice_add_fusion
  (49 shorter events, 6.7 us)
Async XLA Ops:
  0.6 1.3 copy-start
  7.8 7.0 %copy-start.14 = (s32[128]{0:T(128)S(1)}, s32[128]{0:T(128)}, u32[]{:S(2)}) copy-start(s32[128]{0:T(128)} %param.21) | copy-start | bytes 1540
  7.8 34.5 %all-to-all-start = ((bf16[3,4,80,720]{2,1,0,3:T(4,128)(2,1)}), bf16[3,4,80,720]{2,1,0,3:T(4,128)(2,1)S(1)}, u32[]{:S(2)}, u32[]{:S(2)}) async-start(bf16[3,4,80,720]{2,1,0,3:T(4,128)(2,1)} %copy.32), calls=%async_computation | async-start | bytes 4423680 | tf_op jit(solution)/shard_map/all_to_all | solution.py:55
  16.1 33.2 %copy-start.11 = (f32[2]{0:T(128)}, f32[2]{0:T(128)S(1)}, u32[]{:S(2)}) copy-start(f32[2]{0:T(128)S(1)} %dynamic-slice_multiply_fusion) | copy-start | bytes 28
  46.1 5.0 %copy-start.2 = (bf16[2,4,320,180]{2,1,3,0:T(4,128)(2,1)S(1)}, bf16[2,4,320,180]{2,1,3,0:T(4,128)(2,1)}, u32[]{:S(2)}) copy-start(bf16[2,4,320,180]{2,1,3,0:T(4,128)(2,1)} %param.13) | copy-start | bytes 2764804
  49.4 1.7 copy-start.1
  53.0 11.2 %copy-start.15 = (f32[32]{0:T(128)S(1)}, f32[32]{0:T(128)}, u32[]{:S(2)}) copy-start(f32[32]{0:T(128)} %param.20) | copy-start | bytes 388
  53.0 11.7 %copy-start.10 = (s32[5,180]{1,0:T(8,128)S(1)}, s32[5,180]{1,0:T(8,128)}, u32[]{:S(2)}) copy-start(s32[5,180]{1,0:T(8,128)} %param.18) | copy-start | bytes 10804
  53.0 42.4 %all-to-all-start.1 = ((f32[64,4,5,180]{3,1,2,0:T(4,128)}), f32[64,4,5,180]{3,1,2,0:T(4,128)S(1)}, u32[]{:S(2)}, u32[]{:S(2)}) async-start(f32[64,4,5,180]{3,1,2,0:T(4,128)} %bitcast.47), calls=%async_computation.1 | async-start | bytes 2621440 | tf_op jit(solution)/shard_map/all_to_all | solution.py:15
  66.8 1.9 %slice-start = ((f32[3,4,320,180]{2,3,1,0:T(8,128)}), f32[1,4,320,180]{2,3,1,0:T(8,128)S(1)}, s32[]{:S(2)}) async-start(f32[3,4,320,180]{2,3,1,0:T(8,128)} %copy-done.1), calls=%async_computation.4 | async-start | bytes 2260992 | tf_op jit(solution)/shard_map/slice | solution.py:58
  69.6 26.1 %copy-start.9 = (f32[4,5,180]{2,0,1:T(4,128)S(1)}, f32[4,5,180]{2,0,1:T(4,128)}, u32[]{:S(2)}) copy-start(f32[4,5,180]{2,0,1:T(4,128)} %copy.47) | copy-start | bytes 43204
  69.6 26.1 %copy-start.4 = (bf16[32,4,5,180]{3,1,2,0:T(4,128)(2,1)S(1)}, bf16[32,4,5,180]{3,1,2,0:T(4,128)(2,1)}, u32[]{:S(2)}) copy-start(bf16[32,4,5,180]{3,1,2,0:T(4,128)(2,1)} %param.17) | copy-start | bytes 691204
  69.6 26.6 %copy-start.8 = (s32[32,5,180]{2,0,1:T(8,128)S(1)}, s32[32,5,180]{2,0,1:T(8,128)}, u32[]{:S(2)}) copy-start(s32[32,5,180]{2,0,1:T(8,128)} %param.19) | copy-start | bytes 345604
  69.6 26.6 %copy-start.13 = (f32[32]{0:T(128)S(1)}, f32[32]{0:T(128)}, u32[]{:S(2)}) copy-start(f32[32]{0:T(128)} %mul.91) | copy-start | bytes 388
  121.9 1.6 copy-start.3
  121.9 1.6 copy-start.12
  123.5 0.9 copy-start.7
  170.2 2.8 %copy-start.6 = (bf16[4,80,720]{2,1,0:T(8,128)(2,1)S(1)}, bf16[4,80,720]{2,1,0:T(8,128)(2,1)}, u32[]{:S(2)}) copy-start(bf16[4,80,720]{2,1,0:T(8,128)(2,1)} %param.12) | copy-start | bytes 1382404
  173.0 1.6 copy-start.5
where the time goes:
time: 177 us; the launch traced here: 176 us
  blocking collectives  56.8 us (32%)
  waiting for transfers between devices  50.7 us (29%)
  local copies, waits for them, and re-layouts  30.3 us (17%)
  starting transfers between devices  18.1 us (10%)
  matrix products  11.2 us (6%)
  other arithmetic  7.28 us (4%)
    all_to_all x1, blocking collectives, shards(): lax.all_to_all(back_lat, 'band', split_axis=2, concat_axis=3, tiled=True)  32.7 us
    all_to_all x1, waiting for transfers between devices, shards(): lax.all_to_all(along_lon, 'band', split_axis=3, concat_axis=2, tiled=True)  26.2 us
    all_to_all x1, waiting for transfers between devices, sum_at_owner(): lax.all_to_all(pieces, axis, split_axis=0, concat_axis=0, tiled=True)  24.6 us
    all_to_all x1, blocking collectives, from_everyone(): lax.all_to_all(jnp.broadcast_to(x[None], (devices, *x.shape)), axis, 0, 0...  24.1 us
    all_to_all x1, starting transfers between devices, sum_at_owner(): lax.all_to_all(pieces, axis, split_axis=0, concat_axis=0, tiled=True)  11.1 us
    all_to_all x1, starting transfers between devices, shards(): lax.all_to_all(along_lon, 'band', split_axis=3, concat_axis=2, tiled=True)  6.96 us
    convert_element_type x1, local copies, waits for them, and re-layouts, shards(): back_lat = jnp.einsum('ji,msjk->msik', lat_root, adjoints, preferred_elem...  6.66 us
    unnamed x33, local copies, waits for them, and re-layouts  5.99 us
  transfers between devices with their start and end apart: 2, of which 2 were waited for; matrix products, arithmetic and copies ran while one was open for 4% of the time, Pallas kernels for 0%

commit v1 on v0

--- a/solution.py
+++ b/solution.py
@@ -2,6 +2,7 @@
 import jax.numpy as jnp
 from jax import lax
 from jax.sharding import PartitionSpec as P
+from jax.lax import all_to_all, psum
 
 
 def in_blocks(x, dim, devices):
@@ -52,7 +53,15 @@
     own_coef = lax.dynamic_slice_in_dim(coef, rank * members, members, 0)
     fields = jnp.concatenate([alpha, static_ctl[None]], axis=0)
     along_lon = jnp.dot(fields, lon_root, preferred_element_type=jnp.float32).astype(jnp.bfloat16)
-    regrouped = lax.all_to_all(along_lon, "band", split_axis=3, concat_axis=2, tiled=True)
+
+    def _set_samples_all(chunk):
+        wide_out = psum(1, "band")
+        m_next = jnp.split(chunk, wide_out, axis=3)
+        earlier = jnp.stack(m_next, axis=0)
+        all_rows = all_to_all(earlier, "band", 0, 0)
+        return jnp.concatenate(all_rows, axis=2)
+
+    regrouped = _set_samples_all(along_lon)
     along_lat = jnp.einsum("ij,msjk->msik", lat_root, regrouped, preferred_element_type=jnp.float32)
     member_lat = along_lat[:members]
     own_static = lax.dynamic_slice_in_dim(along_lat[members], rank * rows, rows, 1)

time: 177 us -> 169 us (0.955)
  local copies, waits for them, and re-layouts: 30.3 us -> 24.9 us
  waiting for transfers between devices: 50.7 us -> 48.1 us
  other arithmetic: 7.28 us -> 9.1 us
    all_to_all x1 -> x0, local copies, waits for them, and re-layouts: 3.75 us -> none  [shards(): lax.all_to_all(along_lon, 'band', split_axis=3, concat_axis=2, tiled=True)]
    convert_element_type x1 -> x0, local copies, waits for them, and re-layouts: 3.25 us -> none  [shards(): jnp.dot(fields, lon_root, preferred_element_type=jnp.float32)]
    all_to_all x1, waiting for transfers between devices: 26.2 us -> 23.5 us  [_set_samples_all(): all_rows = all_to_all(earlier, 'band', 0, 0)]
    unnamed x33 -> x35, local copies, waits for them, and re-layouts: 5.99 us -> 6.62 us
where the time goes in v1:
time: 169 us; the launch traced here: 168 us
  blocking collectives  56.8 us (34%)
  waiting for transfers between devices  48.1 us (28%)
  local copies, waits for them, and re-layouts  24.9 us (15%)
  starting transfers between devices  18.1 us (11%)
  matrix products  9.62 us (6%)
  other arithmetic  9.1 us (5%)
    all_to_all x1, blocking collectives, shards(): lax.all_to_all(back_lat, 'band', split_axis=2, concat_axis=3, tiled=True)  32.7 us
    all_to_all x1, waiting for transfers between devices, sum_at_owner(): lax.all_to_all(pieces, axis, split_axis=0, concat_axis=0, tiled=True)  24.5 us
    all_to_all x1, blocking collectives, from_everyone(): lax.all_to_all(jnp.broadcast_to(x[None], (devices, *x.shape)), axis, 0, 0...  24.1 us
    all_to_all x1, waiting for transfers between devices, _set_samples_all(): all_rows = all_to_all(earlier, 'band', 0, 0)  23.5 us
    all_to_all x1, starting transfers between devices, sum_at_owner(): lax.all_to_all(pieces, axis, split_axis=0, concat_axis=0, tiled=True)  11.1 us
    all_to_all x1, starting transfers between devices, _set_samples_all(): all_rows = all_to_all(earlier, 'band', 0, 0)  6.94 us
    convert_element_type x1, local copies, waits for them, and re-layouts, shards(): back_lat = jnp.einsum('ji,msjk->msik', lat_root, adjoints, preferred_elem...  6.66 us
    unnamed x35, local copies, waits for them, and re-layouts  6.62 us
  transfers between devices with their start and end apart: 2, of which 2 were waited for; matrix products, arithmetic and copies ran while one was open for 4% of the time, Pallas kernels for 0%

profile of v1, /device:TPU:1, one launch (start us, length us, event | category | flops | bytes accessed | tf_op | source)
XLA Modules:
  0.0 168.2 jit_solution(15087523644420518520)
XLA Ops:
  0.6 1.2 copy-done
  1.9 2.7 %convolution_convert_fusion.1 = bf16[3,4,80,720]{3,2,1,0:T(8,128)(2,1)S(1)} fusion(bf16[1,4,80,720]{3,2,1,0:T(8,128)(2,1)} %bitcast.55, bf16[2,4,80,720]{3,2,1,0:T(8,128)(2,1)} %param.11, bf16[720,720]{1,0:T(8,128)(2,1)S(1)} %copy-done), kind=kOutput, calls=%fused_computation.11 | convolution fusion | flops 996710400 | bytes 3801600 | tf_op jit(solution)/shard_map/dot_general | solution.py:55
  5.2 1.8 %pad_maximum_fusion = bf16[4,3,4,80,180]{4,3,2,1,0:T(8,128)(2,1)} fusion(bf16[1,3,4,80,180]{4,3,2,1,0:T(8,128)(2,1)S(1)} %get-tuple-element.3, bf16[1,3,4,80,180]{4,3,2,1,0:T(8,128)(2,1)S(1)} %get-tuple-element.4, bf16[1,3,4,80,180]{4,3,2,1,0:T(8,128)(2,1)S(1)} %get-tuple-element.5, bf16[1,3,4,80,180]{4,3,2,1,0:T(8,128)(2,1)S(1)} %get-tuple-element.2), kind=kLoop, calls=%fused_computation.5 | loop fusion | flops 2073600 | bytes 2764800 | tf_op jit(solution)/shard_map/stack | solution.py:60
  7.0 6.9 %all-to-all-start = ((bf16[4,3,4,80,180]{4,3,2,1,0:T(8,128)(2,1)}), bf16[4,3,4,80,180]{4,3,2,1,0:T(8,128)(2,1)S(1)}, u32[]{:S(2)}, u32[]{:S(2)}) async-start(bf16[4,3,4,80,180]{4,3,2,1,0:T(8,128)(2,1)} %pad_maximum_fusion), calls=%async_computation | async-start | bytes 3932160 | tf_op jit(solution)/shard_map/all_to_all | solution.py:61
  15.3 23.5 %all-to-all-done = bf16[4,3,4,80,180]{4,3,2,1,0:T(8,128)(2,1)S(1)} async-done(((bf16[4,3,4,80,180]{4,3,2,1,0:T(8,128)(2,1)}), bf16[4,3,4,80,180]{4,3,2,1,0:T(8,128)(2,1)S(1)}, u32[]{:S(2)}, u32[]{:S(2)}) %all-to-all-start) | async-done | bytes 1382432 | tf_op jit(solution)/shard_map/all_to_all | solution.py:61
  39.8 1.6 convolution_bitcast_fusion
  41.5 1.7 %copy-done.1 = f32[3,4,320,180]{2,3,1,0:T(8,128)} copy-done((f32[3,4,320,180]{2,3,1,0:T(8,128)}, f32[3,4,320,180]{2,3,1,0:T(8,128)S(1)}, u32[]{:S(2)}) %copy-start.1) | copy-done | bytes 2764824
  43.6 1.5 copy.33
  45.1 11.1 %all-to-all-start.1 = ((f32[64,4,5,180]{3,1,2,0:T(4,128)}), f32[64,4,5,180]{3,1,2,0:T(4,128)S(1)}, u32[]{:S(2)}, u32[]{:S(2)}) async-start(f32[64,4,5,180]{3,1,2,0:T(4,128)} %bitcast.53), calls=%async_computation.1 | async-start | bytes 2621440 | tf_op jit(solution)/shard_map/all_to_all | solution.py:16
  56.8 2.2 %constant_dynamic-slice_fusion.1 = f32[4,5,180]{1,0,2:T(4,128)} fusion(f32[4,320,180]{1,0,2:T(4,128)} %param.14, s32[]{:T(128)S(6)} %select_n.8), kind=kLoop, calls=%fused_computation.43 | loop fusion | bytes 28804 | tf_op jit(solution)/shard_map/dynamic_slice | solution.py:73
  59.0 1.8 %copy.45 = f32[4,5,180]{2,0,1:T(4,128)} copy(f32[4,5,180]{1,0,2:T(4,128)} %constant_dynamic-slice_fusion.1) | data formatting | bytes 28800
  61.7 1.2 copy.35
  63.0 24.5 %all-to-all-done.1 = f32[64,4,5,180]{3,1,2,0:T(4,128)S(1)} async-done(((f32[64,4,5,180]{3,1,2,0:T(4,128)}), f32[64,4,5,180]{3,1,2,0:T(4,128)S(1)}, u32[]{:S(2)}, u32[]{:S(2)}) %all-to-all-start.1) | async-done | bytes 921632 | tf_op jit(solution)/shard_map/all_to_all | solution.py:16
  88.8 24.1 %all_to_all.33 = bf16[64,4,5,180]{3,1,2,0:T(4,128)(2,1)S(1)} all-to-all(bf16[64,4,5,180]{3,1,2,0:T(4,128)(2,1)S(1)} %broadcast_in_dim.7), channel_id=1, replica_groups=mesh['mem'=64,'band'=4] {'mem'}, dimensions={0} | all-to-all | bytes 921600 | tf_op jit(solution)/shard_map/all_to_all | solution.py:28
  113.1 0.9 copy.36
  114.0 1.5 fusion.18
  116.5 2.5 %fusion.4 = bf16[3,4,320,180]{2,3,1,0:T(8,128)(2,1)} fusion(bf16[1,4,320,180]{2,3,1,0:T(8,128)(2,1)S(1)} %fusion.18, bf16[2,4,320,180]{2,3,1,0:T(8,128)(2,1)S(1)} %multiply_convert_fusion, bf16[320,320]{1,0:T(8,128)(2,1)S(1)} %copy-done.8), kind=kOutput, calls=%fused_computation.12 | convolution fusion | flops 443750400 | bytes 2969600 | tf_op jit(solution)/shard_map/ji,msjk->msik/dot_general | solution.py:89
  119.1 6.7 %copy.39 = bf16[3,4,320,180]{3,1,0,2:T(4,128)(2,1)S(1)} copy(bf16[3,4,320,180]{2,3,1,0:T(8,128)(2,1)} %fusion.4) | data formatting | bytes 2764800 | tf_op jit(solution)/shard_map/convert_element_type | solution.py:91
  125.7 32.7 %all_to_all.34 = bf16[3,4,320,180]{3,1,0,2:T(4,128)(2,1)S(1)} all-to-all(bf16[3,4,320,180]{3,1,0,2:T(4,128)(2,1)S(1)} %copy.39), channel_id=1, replica_groups=mesh['mem'=64,'band'=4] {'band'}, dimensions={2} | all-to-all | bytes 2764800 | tf_op jit(solution)/shard_map/all_to_all | solution.py:92
  158.8 1.0 copy.41
  159.8 2.5 %all_to_all.28 = bf16[3,4,80,720]{3,2,1,0:T(8,128)(2,1)} reshape(bf16[3,4,80,4,180]{4,3,2,1,0:T(4,128)(2,1)S(1)} %copy.41) | data formatting | bytes 2764800 | tf_op jit(solution)/shard_map/all_to_all | solution.py:92
  162.3 2.8 %fusion.12 = f32[3,4,80,720]{3,2,1,0:T(8,128)S(1)} fusion(bf16[3,4,80,720]{3,2,1,0:T(8,128)(2,1)} %all_to_all.28, bf16[720,720]{1,0:T(8,128)(2,1)S(1)} %copy-done), kind=kOutput, calls=%fused_computation.19 | convolution fusion | flops 995328000 | bytes 5184000 | tf_op jit(solution)/shard_map/msil,jl->msij/dot_general | solution.py:93
  165.1 1.0 fusion.15
  166.7 1.5 slice_add_fusion
  (52 shorter events, 7.4 us)
Async XLA Ops:
  0.6 1.3 copy-start
  7.0 6.9 %copy-start.15 = (s32[128]{0:T(128)S(1)}, s32[128]{0:T(128)}, u32[]{:S(2)}) copy-start(s32[128]{0:T(128)} %param.21) | copy-start | bytes 1540
  7.0 31.9 %all-to-all-start = ((bf16[4,3,4,80,180]{4,3,2,1,0:T(8,128)(2,1)}), bf16[4,3,4,80,180]{4,3,2,1,0:T(8,128)(2,1)S(1)}, u32[]{:S(2)}, u32[]{:S(2)}) async-start(bf16[4,3,4,80,180]{4,3,2,1,0:T(8,128)(2,1)} %pad_maximum_fusion), calls=%async_computation | async-start | bytes 3932160 | tf_op jit(solution)/shard_map/all_to_all | solution.py:61
  15.3 26.1 %copy-start.12 = (f32[2]{0:T(128)}, f32[2]{0:T(128)S(1)}, u32[]{:S(2)}) copy-start(f32[2]{0:T(128)S(1)} %dynamic-slice_multiply_fusion) | copy-start | bytes 28
  38.9 0.9 copy-start.7
  39.8 3.4 %copy-start.2 = (bf16[2,4,320,180]{2,1,3,0:T(4,128)(2,1)S(1)}, bf16[2,4,320,180]{2,1,3,0:T(4,128)(2,1)}, u32[]{:S(2)}) copy-start(bf16[2,4,320,180]{2,1,3,0:T(4,128)(2,1)} %param.13) | copy-start | bytes 2764804
  41.5 1.7 %copy-start.1 = (f32[3,4,320,180]{2,3,1,0:T(8,128)}, f32[3,4,320,180]{2,3,1,0:T(8,128)S(1)}, u32[]{:S(2)}) copy-start(f32[3,4,320,180]{2,3,1,0:T(8,128)S(1)} %convolution_bitcast_fusion) | copy-start | bytes 8294404
  45.1 11.2 %copy-start.16 = (f32[32]{0:T(128)S(1)}, f32[32]{0:T(128)}, u32[]{:S(2)}) copy-start(f32[32]{0:T(128)} %param.20) | copy-start | bytes 388
  45.1 11.7 %copy-start.11 = (s32[5,180]{1,0:T(8,128)S(1)}, s32[5,180]{1,0:T(8,128)}, u32[]{:S(2)}) copy-start(s32[5,180]{1,0:T(8,128)} %param.18) | copy-start | bytes 10804
  45.1 42.4 %all-to-all-start.1 = ((f32[64,4,5,180]{3,1,2,0:T(4,128)}), f32[64,4,5,180]{3,1,2,0:T(4,128)S(1)}, u32[]{:S(2)}, u32[]{:S(2)}) async-start(f32[64,4,5,180]{3,1,2,0:T(4,128)} %bitcast.53), calls=%async_computation.1 | async-start | bytes 2621440 | tf_op jit(solution)/shard_map/all_to_all | solution.py:16
  56.8 4.0 %slice-start = ((f32[3,4,320,180]{2,3,1,0:T(8,128)}), f32[1,4,320,180]{2,3,1,0:T(8,128)S(1)}, s32[]{:S(2)}) async-start(f32[3,4,320,180]{2,3,1,0:T(8,128)} %copy-done.1), calls=%async_computation.4 | async-start | bytes 2260992 | tf_op jit(solution)/shard_map/slice | solution.py:67
  61.7 26.0 %copy-start.10 = (f32[4,5,180]{2,0,1:T(4,128)S(1)}, f32[4,5,180]{2,0,1:T(4,128)}, u32[]{:S(2)}) copy-start(f32[4,5,180]{2,0,1:T(4,128)} %copy.45) | copy-start | bytes 43204
  61.7 26.1 %copy-start.4 = (bf16[32,4,5,180]{3,1,2,0:T(4,128)(2,1)S(1)}, bf16[32,4,5,180]{3,1,2,0:T(4,128)(2,1)}, u32[]{:S(2)}) copy-start(bf16[32,4,5,180]{3,1,2,0:T(4,128)(2,1)} %param.17) | copy-start | bytes 691204
  61.7 26.5 %copy-start.9 = (s32[32,5,180]{2,0,1:T(8,128)S(1)}, s32[32,5,180]{2,0,1:T(8,128)}, u32[]{:S(2)}) copy-start(s32[32,5,180]{2,0,1:T(8,128)} %param.19) | copy-start | bytes 345604
  61.7 26.5 %copy-start.14 = (f32[32]{0:T(128)S(1)}, f32[32]{0:T(128)}, u32[]{:S(2)}) copy-start(f32[32]{0:T(128)} %mul.91) | copy-start | bytes 388
  114.0 1.6 copy-start.3
  114.0 1.6 copy-start.13
  115.6 0.9 copy-start.8
  162.3 2.8 %copy-start.6 = (bf16[4,80,720]{2,1,0:T(8,128)(2,1)S(1)}, bf16[4,80,720]{2,1,0:T(8,128)(2,1)}, u32[]{:S(2)}) copy-start(bf16[4,80,720]{2,1,0:T(8,128)(2,1)} %param.12) | copy-start | bytes 1382404
  165.1 1.6 copy-start.5
